TPU v7x, 256 devices: a whole 4x4x8 slice. The times are simulated.
256 devices in a mesh: row: 32 (over z, x), feat: 8 (over y, core).
Axes of the slice: x: 4, y: 4, z: 8, core: 2. Of those that a mesh axis runs over, the one named last changes fastest.
Arguments:
- bin_codes: int32 [256, 262144], P(None, 'row'), may hold values from 0 to 31
- gradients: bfloat16 [262144], P('row'), may hold values from -6 to 6
- hessians: bfloat16 [262144], P('row'), may hold values from 0.019897461 to 0.25
- pair_list: int32 [64, 2], replicated, may hold values from 0 to 255, as said below
- owners: int32 [64], replicated, may hold values from 0 to 7, as said below
Outputs:
- cut_table: float32 [128, 1024], P('feat', 'row')
- best_gain: float32 [64], replicated
Inputs may be any that keep to these rules, and one draw needn't show every extreme that they name: `pair_list`: each row holds two different features, the first smaller. `owners`: one index owns exactly 16 pairs in every draw, the others at most that many.
All inputs are finite; a program needn't handle non-finite values.
Results may differ from a plain program's by a relative error of at most 0.0003.
Values sent between devices are 32-bit elements; how exact they have to be, the bound alone decides.
A program may use at most 64 MiB of HBM per device.

v0:
```python
import jax
import jax.numpy as jnp
from jax import lax
from jax.sharding import PartitionSpec as P

BINS = 32
LAMBDA_REG = 1.0


def slot_rank(owners):
    pair_ids = jnp.arange(owners.shape[0], dtype=jnp.int32)
    same_owner = owners[:, None] == owners[None, :]
    earlier = pair_ids[None, :] < pair_ids[:, None]
    return jnp.sum((same_owner & earlier).astype(jnp.int32), axis=1)


def cumulate(histogram):
    bin_count = histogram.shape[-2]
    running = jnp.cumsum(histogram, axis=-2)
    shaped = running.reshape(running.shape[:-1] + (2, bin_count))
    shaped = jnp.cumsum(shaped, axis=-1)
    return shaped.reshape(running.shape)


def cut_gains(cut_rows, margin_row):
    bin_count = margin_row.shape[-1] // 2
    grad_cum = cut_rows[..., :bin_count]
    hess_cum = cut_rows[..., bin_count:]
    grad_end = grad_cum[..., -1:]
    hess_end = hess_cum[..., -1:]
    grad_col = margin_row[..., None, :bin_count]
    hess_col = margin_row[..., None, bin_count:]
    grad_all = margin_row[..., None, bin_count - 1 : bin_count]
    hess_all = margin_row[..., None, 2 * bin_count - 1 :]
    quad_grad = (
        grad_cum,
        grad_end - grad_cum,
        grad_col - grad_cum,
        grad_all - grad_end - grad_col + grad_cum,
    )
    quad_hess = (
        hess_cum,
        hess_end - hess_cum,
        hess_col - hess_cum,
        hess_all - hess_end - hess_col + hess_cum,
    )
    result = -(grad_all * grad_all) / (hess_all + LAMBDA_REG)
    for grad_part, hess_part in zip(quad_grad, quad_hess):
        result = result + grad_part * grad_part / (hess_part + LAMBDA_REG)
    return result


def shards(bin_codes, gradients, hessians, pair_list, owners):
    feat_count = lax.axis_size("feat")
    row_count = lax.axis_size("row")
    feat_index = lax.axis_index("feat")
    row_index = lax.axis_index("row")
    pair_count = pair_list.shape[0]
    bin_count = BINS
    row_share = bin_count // row_count
    home_slots = 2 * pair_count // feat_count
    rank = slot_rank(owners)
    pair_ids = jnp.arange(pair_count, dtype=jnp.int32)
    places = jnp.arange(home_slots, dtype=jnp.int32)
    matched = (owners[None, :] == feat_index) & (rank[None, :] == places[:, None])
    chosen = jnp.sum(jnp.where(matched, pair_ids[None, :], 0), axis=1)
    present = jnp.any(matched, axis=1)
    lookup = owners * home_slots + rank
    chosen_pairs = pair_list[chosen]
    picked = jnp.take(bin_codes, chosen_pairs.reshape(-1), axis=0)
    picked = picked.reshape(home_slots, 2, -1)
    levels = jnp.arange(bin_count, dtype=jnp.int32)
    hot_first = (picked[:, 0, None, :] == levels[None, :, None]).astype(jnp.bfloat16)
    hot_second = (picked[:, 1, None, :] == levels[None, :, None]).astype(jnp.bfloat16)
    weighted = jnp.concatenate(
        [hot_second * gradients[None, None, :], hot_second * hessians[None, None, :]], axis=1
    )
    histogram = jnp.einsum("sar,sxr->sax", hot_first, weighted, preferred_element_type=jnp.float32)
    histogram = histogram * present[:, None, None].astype(jnp.float32)
    summed = lax.psum(histogram, "row")
    running = cumulate(summed)
    cut_rows = lax.dynamic_slice_in_dim(running, row_index * row_share, row_share, 1)
    margin_row = running[:, -1, :]
    cut_gain = cut_gains(cut_rows, margin_row).reshape(home_slots, row_share * bin_count)
    row_peak = lax.pmax(jnp.max(cut_gain, axis=1), "row")
    everyone = lax.all_gather(row_peak, "feat", axis=0, tiled=True)
    best_gain = everyone[lookup]
    return (cut_gain, best_gain)


def solution(mesh):
    in_specs = (P(None, "row"), P("row"), P("row"), P(), P())
    out_specs = (P("feat", "row"), P())
    return jax.shard_map(shards, mesh=mesh, in_specs=in_specs, out_specs=out_specs, check_vma=False)
```

profile of v0, /device:TPU:1, one launch (start us, length us, event | category | flops | bytes accessed | tf_op | source)
XLA Modules:
  0.0 291.0 jit_solution(3564876768124046581)
XLA Ops:
  7.2 0.0 copy-start
  7.2 0.0 copy-start.1
  7.2 0.0 all-reduce.3.cloned.1.call-start
  7.2 0.9 convert_reduce_fusion
  8.1 0.7 broadcast_compare_fusion
  8.8 0.1 select_reduce_fusion
  9.0 0.8 copy.58
  9.7 0.6 gather_fusion
  10.3 0.1 reshape.114
  10.4 0.1 fusion.23
  10.5 4.7 %gather_fusion.1 = s32[32,8192]{1,0:T(8,128)S(1)} fusion(s32[256,8192]{1,0:T(8,128)} %param.5, s32[1024]{0:T(1024)S(1)} %pad_clamp_fusion.1), kind=kCustom, calls=%fused_computation.1 | custom fusion | bytes 2097280 | tf_op jit(solution)/shard_map/jit(_take)/gather | solution.py:70
  15.3 0.6 gather.14
  15.9 0.1 copy.59
  16.0 0.7 copy_select_fusion
  16.7 0.1 slice_bitcast_fusion.1
  16.8 0.0 copy-done
  16.8 0.0 copy-done.1
  16.8 9.2 %fusion.5 = (bf16[16,32,8192]{2,1,0:T(8,128)(2,1)}, bf16[16,32,8192]{2,1,0:T(8,128)(2,1)}) fusion(s32[16,8192]{1,0:T(8,128)S(1)} %get-tuple-element.11, bf16[8192]{0:T(1024)(128)(2,1)S(1)} %copy-done, bf16[8192]{0:T(1024)(128)(2,1)S(1)} %copy-done.1), kind=kLoop, calls=%fused_computation.9 | loop fusion | flops 12582912 | bytes 17334272 | tf_op jit(solution)/shard_map/mul | solution.py:76
  26.0 0.0 copy-start.2
  26.0 0.0 copy-start.3
  26.0 8.4 %fusion.7 = f32[16,32,64]{2,1,0:T(8,128)S(1)} fusion(bf16[16,32,8192]{2,1,0:T(8,128)(2,1)} %get-tuple-element.13, bf16[16,32,8192]{2,1,0:T(8,128)(2,1)} %get-tuple-element.12, s32[16,8192]{1,0:T(8,128)S(1)} %get-tuple-element.10, f32[16]{0:T(128)S(1)} %convert_element_type.14), kind=kOutput, calls=%fused_computation.12 | convolution fusion | flops 574652416 | bytes 17432640 | tf_op jit(solution)/shard_map/sar,sxr->sax/dot_general | solution.py:78
  34.3 0.3 reduce_window_sum.24
  34.7 1.1 copy.61
  35.8 0.0 all-reduce.3.cloned.1.call-update
  35.8 0.0 copy-done.2
  35.8 0.0 copy-done.3
  35.8 0.6 dynamic-slice
  37.1 146.9 %all-reduce.3.cloned.1.call-done = f32[16,32,2,32]{3,0,1,2:T(8,128)} async-done(((f32[16,32,2,32]{3,0,1,2:T(8,128)}), f32[16,32,2,32]{3,0,1,2:T(8,128)}) %all-reduce.3.cloned.1.call-update) | async-done | bytes 131088 | tf_op jit(solution)/shard_map/psum | solution.py:80
  184.0 1.1 fusion.29
  185.1 0.2 copy.62
  185.2 6.1 %reduce_window_sum.26 = f32[16,32,2,32]{3,1,2,0:T(8,128)S(1)} reduce-window(f32[16,32,2,32]{3,1,2,0:T(8,128)S(1)} %copy.62, f32[]{:T(128)} %constant.45.clone.1), window={size=1x1x1x32 pad=0_0x0_0x0_0x31_0}, to_apply=%region_5.6 | reduce-window | flops 1015808 | bytes 262148 | tf_op jit(solution)/shard_map/jit(cumsum)/reduce_window_sum | solution.py:21
  191.4 0.4 copy.68
  191.8 0.3 reshape.147
  192.1 0.2 fusion.21
  192.3 0.2 fusion.16
  192.5 0.8 fusion.27
  193.3 58.4 %pmax.7 = f32[16]{0:T(128)S(1)} all-reduce(f32[16]{0:T(128)S(1)} %get-tuple-element.8), channel_id=1, replica_groups=mesh['row'=32,'feat'=8] {'row'}, use_global_device_ids=true, to_apply=%region_7.8 | all-reduce | flops 16 | bytes 128 | tf_op jit(solution)/shard_map/pmax | solution.py:85
  251.8 0.2 dynamic-update-slice
  252.0 30.9 %all-reduce = f32[128]{0:T(128)S(1)} all-reduce(f32[128]{0:T(128)S(1)} %dynamic-update-slice), channel_id=1, replica_groups=mesh['row'=32,'feat'=8] {'feat'}, use_global_device_ids=true, to_apply=%add | all-reduce | flops 128 | bytes 1024
  282.9 1.3 gather_fusion.2
  (10 shorter events, 0.1 us)
Async XLA Ops:
  7.2 9.6 %copy-start = (bf16[8192]{0:T(1024)(128)(2,1)S(1)}, bf16[8192]{0:T(1024)(128)(2,1)}, u32[]{:S(2)}) copy-start(bf16[8192]{0:T(1024)(128)(2,1)} %param.6) | copy-start | bytes 49156
  7.2 9.6 %copy-start.1 = (bf16[8192]{0:T(1024)(128)(2,1)S(1)}, bf16[8192]{0:T(1024)(128)(2,1)}, u32[]{:S(2)}) copy-start(bf16[8192]{0:T(1024)(128)(2,1)} %param.7) | copy-start | bytes 49156
  7.2 176.8 %all-reduce.3.cloned.1.call-start = ((), (), s32[]{:S(2)}) async-start(), calls=%async_computation | async-start | bytes 1048576 | tf_op jit(solution)/shard_map/psum | solution.py:80
  26.0 9.8 %copy-start.2 = (s32[64]{0:T(128)S(1)}, s32[64]{0:T(128)}, u32[]{:S(2)}) copy-start(s32[64]{0:T(128)} %param.9) | copy-start | bytes 772
  26.0 9.9 %copy-start.3 = (u32[256]{0:T(256)S(1)}, u32[256]{0:T(256)}, u32[]{:S(2)}) copy-start(u32[256]{0:T(256)} %constant.55) | copy-start | bytes 3076
Sparse Core Ops, SparseCore 0:
  35.9 148.0 all-reduce.2
where the time goes:
time: 291 us
  waiting for transfers between devices  147 us (51%)
  blocking collectives  89.3 us (31%)
  other arithmetic  20.2 us (7%)
  between operations  14.9 us (5%)
  local copies, waits for them, and re-layouts  11.4 us (4%)
  matrix products  8.35 us (3%)
    psum x1, waiting for transfers between devices, shards(): summed = lax.psum(histogram, 'row')  147 us
    pmax x1, blocking collectives, shards(): row_peak = lax.pmax(jnp.max(cut_gain, axis=1), 'row')  58.4 us
    unnamed x1, blocking collectives  30.9 us
    mul x1, other arithmetic, shards(): hot_second * gradients[None, None, :]  9.18 us
    dot_general x1, matrix products, shards(): jnp.einsum('sar,sxr->sax', hot_first, weighted, preferred_element_type=jn...  8.35 us
    another operation x1, other arithmetic, cumulate(): shaped = jnp.cumsum(shaped, axis=-1)  6.13 us
  transfers between devices with their start and end apart: 1, of which 1 were waited for; matrix products, arithmetic and copies ran while one was open for 0% of the time, Pallas kernels for 0%

commit v1 on v0

--- a/solution.py
+++ b/solution.py
@@ -77,7 +77,7 @@
     )
     histogram = jnp.einsum("sar,sxr->sax", hot_first, weighted, preferred_element_type=jnp.float32)
     histogram = histogram * present[:, None, None].astype(jnp.float32)
-    summed = lax.psum(histogram, "row")
+    summed = jnp.sum(lax.all_gather(histogram, "row"), axis=0)
     running = cumulate(summed)
     cut_rows = lax.dynamic_slice_in_dim(running, row_index * row_share, row_share, 1)
     margin_row = running[:, -1, :]

time: 291 us -> 243 us (0.84)
  waiting for transfers between devices: 147 us -> 99.8 us
  blocking collectives: 89.3 us -> 84.4 us
  other arithmetic: 20.2 us -> 23.9 us
    psum x1 -> x0, waiting for transfers between devices: 147 us -> none  [shards(): summed = lax.psum(histogram, 'row')]
    all_gather x0 -> x1, waiting for transfers between devices: none -> 99.7 us  [shards(): summed = jnp.sum(lax.all_gather(histogram, 'row'), axis=0)]
    reduce_sum x0 -> x1, other arithmetic: none -> 4.46 us  [shards(): summed = jnp.sum(lax.all_gather(histogram, 'row'), axis=0)]
    unnamed x1, blocking collectives: 30.9 us -> 27.3 us
where the time goes in v1:
time: 243 us; the launch traced here: 242 us
  waiting for transfers between devices  99.8 us (41%)
  blocking collectives  84.4 us (35%)
  other arithmetic  23.9 us (10%)
  between operations  14.9 us (6%)
  local copies, waits for them, and re-layouts  10.3 us (4%)
  matrix products  9.1 us (4%)
    all_gather x1, waiting for transfers between devices, shards(): summed = jnp.sum(lax.all_gather(histogram, 'row'), axis=0)  99.7 us
    pmax x1, blocking collectives, shards(): row_peak = lax.pmax(jnp.max(cut_gain, axis=1), 'row')  57.1 us
    unnamed x1, blocking collectives  27.3 us
    mul x1, other arithmetic, shards(): hot_second * gradients[None, None, :]  9.18 us
    dot_general x1, matrix products, shards(): jnp.einsum('sar,sxr->sax', hot_first, weighted, preferred_element_type=jn...  9.1 us
    another operation x1, other arithmetic, cumulate(): shaped = jnp.cumsum(shaped, axis=-1)  6.13 us
    gather x2, local copies, waits for them, and re-layouts, shards(): picked = jnp.take(bin_codes, chosen_pairs.reshape(-1), axis=0)  5.36 us
  transfers between devices with their start and end apart: 1, of which 1 were waited for; matrix products, arithmetic and copies ran while one was open for 0% of the time, Pallas kernels for 0%

profile of v1, /device:TPU:1, one launch (start us, length us, event | category | flops | bytes accessed | tf_op | source)
XLA Modules:
  0.0 242.3 jit_solution(18271233300120912534)
XLA Ops:
  7.2 0.0 copy-start
  7.2 0.0 copy-start.1
  7.2 0.0 all-gather.3.cloned.1.call-start
  7.2 0.9 convert_reduce_fusion
  8.1 0.7 broadcast_compare_fusion
  8.8 0.1 select_reduce_fusion
  9.0 0.8 copy.72
  9.7 0.6 gather_fusion
  10.3 0.1 reshape.114
  10.4 0.1 fusion.25
  10.5 4.7 %gather_fusion.1 = s32[32,8192]{1,0:T(8,128)S(1)} fusion(s32[256,8192]{1,0:T(8,128)} %param.5, s32[1024]{0:T(1024)S(1)} %pad_clamp_fusion.1), kind=kCustom, calls=%fused_computation.1 | custom fusion | bytes 2097280 | tf_op jit(solution)/shard_map/jit(_take)/gather | solution.py:70
  15.3 0.6 gather.14
  15.9 0.1 copy.73
  16.0 0.7 copy_select_fusion
  16.7 0.1 slice_bitcast_fusion.1
  16.8 0.0 copy-done
  16.8 0.0 copy-done.1
  16.8 9.2 %fusion.5 = (bf16[16,32,8192]{2,1,0:T(8,128)(2,1)}, bf16[16,32,8192]{2,1,0:T(8,128)(2,1)}) fusion(s32[16,8192]{1,0:T(8,128)S(1)} %get-tuple-element.11, bf16[8192]{0:T(1024)(128)(2,1)S(1)} %copy-done, bf16[8192]{0:T(1024)(128)(2,1)S(1)} %copy-done.1), kind=kLoop, calls=%fused_computation.9 | loop fusion | flops 12582912 | bytes 17334272 | tf_op jit(solution)/shard_map/mul | solution.py:76
  26.0 0.0 copy-start.3
  26.0 0.0 copy-start.2
  26.0 9.1 %fusion.7 = f32[16,32,64]{2,1,0:T(8,128)} fusion(bf16[16,32,8192]{2,1,0:T(8,128)(2,1)} %get-tuple-element.13, bf16[16,32,8192]{2,1,0:T(8,128)(2,1)} %get-tuple-element.12, s32[16,8192]{1,0:T(8,128)S(1)} %get-tuple-element.10, f32[16]{0:T(128)S(1)} %convert_element_type.14), kind=kOutput, calls=%fused_computation.12 | convolution fusion | flops 574652416 | bytes 17432640 | tf_op jit(solution)/shard_map/sar,sxr->sax/dot_general | solution.py:78
  35.1 0.0 all-gather.3.cloned.1.call-update
  35.1 0.0 copy-done.3
  35.1 0.6 dynamic-slice
  36.3 0.0 copy-done.2
  36.4 99.7 %all-gather.3.cloned.1.call-done = f32[512,32,64]{2,1,0:T(8,128)} async-done(((f32[16,32,64]{2,1,0:T(8,128)}), f32[512,32,64]{2,1,0:T(8,128)}) %all-gather.3.cloned.1.call-update) | async-done | bytes 4194320 | tf_op jit(solution)/shard_map/all_gather | solution.py:80
  136.1 4.5 %reduce_sum.32 = f32[16,32,64]{2,1,0:T(8,128)S(1)} reduce(f32[32,16,32,64]{3,2,1,0:T(8,128)} %bitcast.59, f32[]{:T(128)} %constant.46.clone.1), dimensions={0}, to_apply=%region_3.4 | reduce | flops 1015808 | bytes 4325380 | tf_op jit(solution)/shard_map/reduce_sum | solution.py:80
  140.6 0.3 reduce_window_sum.24
  140.9 0.4 fusion.10
  141.3 0.2 copy.76
  141.5 6.1 %reduce_window_sum.26 = f32[16,32,2,32]{3,1,2,0:T(8,128)S(1)} reduce-window(f32[16,32,2,32]{3,1,2,0:T(8,128)S(1)} %copy.76, f32[]{:T(128)} %constant.46.clone.1), window={size=1x1x1x32 pad=0_0x0_0x0_0x31_0}, to_apply=%region_5.6 | reduce-window | flops 1015808 | bytes 262148 | tf_op jit(solution)/shard_map/jit(cumsum)/reduce_window_sum | solution.py:21
  147.6 0.4 copy.82
  148.0 0.3 reshape.148
  148.3 0.2 fusion.23
  148.5 0.2 fusion.18
  148.8 0.8 fusion.29
  149.6 57.1 %pmax.7 = f32[16]{0:T(128)S(1)} all-reduce(f32[16]{0:T(128)S(1)} %get-tuple-element.8), channel_id=1, replica_groups=mesh['row'=32,'feat'=8] {'row'}, use_global_device_ids=true, to_apply=%region_7.8 | all-reduce | flops 16 | bytes 128 | tf_op jit(solution)/shard_map/pmax | solution.py:85
  206.6 0.2 dynamic-update-slice
  206.9 27.3 %all-reduce = f32[128]{0:T(128)S(1)} all-reduce(f32[128]{0:T(128)S(1)} %dynamic-update-slice), channel_id=1, replica_groups=mesh['row'=32,'feat'=8] {'feat'}, use_global_device_ids=true, to_apply=%add | all-reduce | flops 128 | bytes 1024
  234.2 1.3 gather_fusion.2
  (10 shorter events, 0.1 us)
Async XLA Ops:
  7.2 9.6 %copy-start = (bf16[8192]{0:T(1024)(128)(2,1)S(1)}, bf16[8192]{0:T(1024)(128)(2,1)}, u32[]{:S(2)}) copy-start(bf16[8192]{0:T(1024)(128)(2,1)} %param.6) | copy-start | bytes 49156
  7.2 9.6 %copy-start.1 = (bf16[8192]{0:T(1024)(128)(2,1)S(1)}, bf16[8192]{0:T(1024)(128)(2,1)}, u32[]{:S(2)}) copy-start(bf16[8192]{0:T(1024)(128)(2,1)} %param.7) | copy-start | bytes 49156
  7.2 128.9 %all-gather.3.cloned.1.call-start = ((), (), s32[]{:S(2)}) async-start(), calls=%async_computation | async-start | bytes 8650752 | tf_op jit(solution)/shard_map/all_gather | solution.py:80
  26.0 9.1 %copy-start.3 = (u32[256]{0:T(256)S(1)}, u32[256]{0:T(256)}, u32[]{:S(2)}) copy-start(u32[256]{0:T(256)} %constant.56) | copy-start | bytes 3076
  26.0 10.4 %copy-start.2 = (s32[64]{0:T(128)S(1)}, s32[64]{0:T(128)}, u32[]{:S(2)}) copy-start(s32[64]{0:T(128)} %param.9) | copy-start | bytes 772
Sparse Core Ops, SparseCore 0:
  35.2 100.8 all-gather.2
